TPU v7x, 32 devices: a whole 2x2x4 slice. The times are simulated.
32 devices in a mesh: gx: 8 (over z, y), gy: 4 (over x, core).
Axes of the slice: x: 2, y: 2, z: 4, core: 2. Of those that a mesh axis runs over, the one named last changes fastest.
Arguments:
- fields: float32 [6, 128, 96, 128], P(None, 'gx', 'gy'), may hold values from -6 to 6
- material: int32 [128, 96, 128], P('gx', 'gy'), may hold values from 0 to 15
- permittivity: float32 [16], replicated, may hold values from 1 to 4
- patch_cell: int32 [8192], P(('gx', 'gy')), may hold values from 0 to 49151
- patch_owner: int32 [8192, 1], P(('gx', 'gy')), may hold values from 0 to 31; in each aligned block of 256 rows (0 to 255, 256 to 511, ...) at most 16 rows name the same one
Outputs:
- new_fields: float32 [6, 128, 96, 128], P(None, 'gx', 'gy')
- far_field: float32 [12, 4096], P(None, ('gx', 'gy'))
Inputs may be any that keep to these rules, and one draw needn't show every extreme that they name: `patch_cell`: an index into the cells of the patch's own device block, x slowest and z fastest. `patch_owner`: among the rows of one device no sector is named by more than 16 rows, a bound that some block reaches; every sector is named by some row.
All inputs are finite; a program needn't handle non-finite values.
Results may differ from a plain program's by a relative error of at most 0.00022.
Values sent between devices are 32-bit elements; how exact they have to be, the bound alone decides.
A program may use at most 128 MiB of HBM per device.

v0:
```python
import functools
import math

import jax
import jax.numpy as jnp
from jax import lax
from jax.experimental import pallas as pl
from jax.experimental.pallas import tpu as pltpu
from jax.sharding import PartitionSpec as P

ANG_DEV = 128
COURANT = 64
KAPPA = 0.5
MESH = pl.DeviceIdType.MESH
Y_MEMBERS = (0, 2, 3, 5)
CHUNKS = ((0, 2), (2, 2), (4, 2))


def slope_rows(value, low_row, high_row):
    rows = value.shape[0]
    at = lax.broadcasted_iota(jnp.int32, value.shape, 0)
    below = jnp.where(at == 0, low_row, pltpu.roll(value, 1, 0))
    above = jnp.where(at == rows - 1, high_row, pltpu.roll(value, rows - 1, 0))
    return 0.5 * (above - below)


def slope_lanes(value):
    lanes = value.shape[1]
    at = lax.broadcasted_iota(jnp.int32, value.shape, 1)
    below = jnp.where(at == 0, 0.0, pltpu.roll(value, 1, 1))
    above = jnp.where(at == lanes - 1, 0.0, pltpu.roll(value, lanes - 1, 1))
    return 0.5 * (above - below)


def updated(centre, slope_x, slope_y, curl_coef, half_step):
    slope_z = lambda member: slope_lanes(centre[member])
    curl_h = [slope_y(5) - slope_z(4), slope_z(3) - slope_x(5), slope_x(4) - slope_y(3)]
    curl_e = [slope_y(2) - slope_z(1), slope_z(0) - slope_x(2), slope_x(1) - slope_y(0)]
    return [centre[m] + curl_coef * curl_h[m] for m in range(3)] + [
        centre[3 + m] - half_step * curl_e[m] for m in range(3)
    ]


def factor(length, coef_at, gain_ref, pivot_ref, left_ref, right_ref):
    zero = jnp.zeros(gain_ref.shape[1:], jnp.float32)

    def forward(i, carry):
        gain_prev, left_prev = carry
        coef = coef_at(i)
        pivot = 1.0 / (1.0 + 2.0 * coef - coef * gain_prev)
        gain = coef * pivot
        left = gain * left_prev
        gain_ref[i] = gain
        pivot_ref[i] = pivot
        left_ref[i] = left
        return gain, left

    lax.fori_loop(0, length, forward, (zero, jnp.ones_like(zero)))

    def backward(k, carry):
        left_next, right_next = carry
        i = length - 1 - k
        gain = gain_ref[i]
        left = left_ref[i] + gain * left_next
        right = gain * right_next
        left_ref[i] = left
        right_ref[i] = right
        return left, right

    lax.fori_loop(0, length, backward, (zero, jnp.ones_like(zero)))


def sweep_back(length, gain_ref, solved_ref):
    def backward(k, carry):
        i = length - 1 - k
        gain = gain_ref[i]
        now = [solved_ref[m, i] + gain * carry[m] for m in range(6)]
        for m in range(6):
            solved_ref[m, i] = now[m]
        return tuple(now)

    zero = jnp.zeros(gain_ref.shape[1:], jnp.float32)
    lax.fori_loop(0, length, backward, (zero,) * 6)


class Line:
    def __init__(self, axis, count, refs):
        (self.mat_out, self.mat_in, self.rhs_out, self.rhs_in, self.plan, self.gains, self.ends,
         self.mat_sems, self.rhs_sems) = refs
        self.axis = axis
        self.count = count
        self.steps = count.bit_length() - 1
        self.me = lax.axis_index(axis)

    def near(self, k):
        return 1 - (self.me // 2**k) % 2

    def partner(self, k):
        return {self.axis: self.me + (2 * self.near(k) - 1) * 2**k}

    def mat_copy(self, k):
        return pltpu.make_async_remote_copy(
            self.mat_out.at[k], self.mat_in.at[k], self.mat_sems.at[0, k], self.mat_sems.at[1, k],
            device_id=self.partner(k), device_id_type=MESH)

    def rhs_copy(self, k, j):
        first, size = CHUNKS[j]
        if k == self.steps - 1:
            source = self.rhs_out.at[k, self.near(k), pl.ds(first, size)]
            target = self.rhs_in.at[k, 0, pl.ds(first, size)]
        else:
            source = self.rhs_out.at[k, :, pl.ds(first, size)]
            target = self.rhs_in.at[k, :, pl.ds(first, size)]
        return pltpu.make_async_remote_copy(
            source, target, self.rhs_sems.at[0, k, j], self.rhs_sems.at[1, k, j],
            device_id=self.partner(k), device_id_type=MESH)

    def mat_start(self, left_ref, right_ref):
        last = left_ref.shape[0] - 1
        for end, at in ((0, 0), (1, last)):
            self.mat_out[0, 2 * end] = left_ref[at]
            self.mat_out[0, 2 * end + 1] = right_ref[at]
        one, zero = jnp.ones(left_ref.shape[1:], jnp.float32), jnp.zeros(left_ref.shape[1:], jnp.float32)
        self.gains[0] = one
        self.gains[1] = zero
        self.gains[2] = zero
        self.gains[3] = one
        self.mat_copy(0).start()

    def mat_merge(self, k):
        self.mat_copy(k).wait_recv()
        n = self.near(k)
        f = 1 - n
        mine = lambda end, side: self.mat_out[k, 2 * end + side]
        other = lambda end, side: self.mat_in[k, 2 * end + side]
        m_nn, m_fn, m_nf, m_ff = mine(n, n), mine(f, n), mine(n, f), mine(f, f)
        o_nn, o_fn, o_nf, o_ff = other(f, f), other(n, f), other(f, n), other(n, n)
        inv = 1.0 / (1.0 - m_nn * o_nn)
        o_by_m = o_nn * m_nf * inv
        o_by_o = o_nf * inv
        m_by_m = m_nf * inv
        m_by_o = m_nn * o_nf * inv
        gain_in, gain_out = self.gains[n], self.gains[2 + n]
        for slot, value in enumerate((inv, o_nn * inv, m_nn * inv, m_fn, o_fn, gain_in, gain_out)):
            self.plan[k, slot] = value
        if k < self.steps - 1:
            self.mat_out[k + 1, 2 * f + f] = m_ff + m_fn * o_by_m
            self.mat_out[k + 1, 2 * f + n] = m_fn * o_by_o
            self.mat_out[k + 1, 2 * n + n] = o_ff + o_fn * m_by_o
            self.mat_out[k + 1, 2 * n + f] = o_fn * m_by_m
            self.mat_copy(k + 1).start()
            self.gains[f] = self.gains[f] + gain_in * o_by_m
            self.gains[2 + f] = self.gains[2 + f] + gain_out * o_by_m
            self.gains[n] = gain_in * o_by_o
            self.gains[2 + n] = gain_out * o_by_o

    def rhs_start(self, solved_ref):
        last = solved_ref.shape[1] - 1
        for j, (first, size) in enumerate(CHUNKS):
            for m in range(first, first + size):
                self.rhs_out[0, 0, m] = solved_ref[m, 0]
                self.rhs_out[0, 1, m] = solved_ref[m, last]
            self.rhs_copy(0, j).start()

    def rhs_merge(self, k, j):
        first, size = CHUNKS[j]
        self.rhs_copy(k, j).wait_recv()
        n = self.near(k)
        f = 1 - n
        ending = k == self.steps - 1
        inv, o_nn, m_nn, m_fn, o_fn, gain_in, gain_out = [self.plan[k, slot] for slot in range(7)]
        for m in range(first, first + size):
            mine = self.rhs_out[k, n, m]
            other = self.rhs_in[k, 0, m] if ending else self.rhs_in[k, f, m]
            o_value = other * inv + o_nn * mine
            if not ending:
                m_value = mine * inv + m_nn * other
                self.rhs_out[k + 1, f, m] = self.rhs_out[k, f, m] + m_fn * o_value
                self.rhs_out[k + 1, n, m] = self.rhs_in[k, n, m] + o_fn * m_value
            into, out_of = gain_in * o_value, gain_out * o_value
            if k > 0:
                into, out_of = self.ends[0, m] + into, self.ends[1, m] + out_of
            self.ends[0, m] = into
            self.ends[1, m] = out_of
        if not ending:
            self.rhs_copy(k + 1, j).start()

    def drain(self):
        for k in range(self.steps):
            self.mat_copy(k).wait_send()
            for j in range(len(CHUNKS)):
                self.rhs_copy(k, j).wait_send()


def both_ways(axis, count, out_low, out_high, in_low, in_high, sems):
    me = lax.axis_index(axis)
    up = lambda: pltpu.make_async_remote_copy(
        out_high, in_low, sems.at[0], sems.at[1], device_id={axis: me + 1}, device_id_type=MESH)
    down = lambda: pltpu.make_async_remote_copy(
        out_low, in_high, sems.at[2], sems.at[3], device_id={axis: me - 1}, device_id_type=MESH)

    def start():
        @pl.when(me < count - 1)
        def _():
            up().start()

        @pl.when(me > 0)
        def _():
            down().start()

        @pl.when(me == 0)
        def _():
            in_low[...] = jnp.zeros(in_low.shape, jnp.float32)

        @pl.when(me == count - 1)
        def _():
            in_high[...] = jnp.zeros(in_high.shape, jnp.float32)

    def wait():
        @pl.when(me > 0)
        def _():
            up().wait_recv()

        @pl.when(me < count - 1)
        def _():
            down().wait_recv()

    def drain():
        @pl.when(me < count - 1)
        def _():
            up().wait_send()

        @pl.when(me > 0)
        def _():
            down().wait_send()

    return start, wait, drain


def greet(axis, count, barrier):
    me = lax.axis_index(axis)

    @pl.when(me > 0)
    def _():
        pl.semaphore_signal(barrier, inc=1, device_id={axis: me - 1}, device_id_type=MESH)

    @pl.when(me < count - 1)
    def _():
        pl.semaphore_signal(barrier, inc=1, device_id={axis: me + 1}, device_id_type=MESH)

    steps = count.bit_length() - 1
    for k in range(1, steps):
        side = 1 - 2 * ((me // 2**k) % 2)
        pl.semaphore_signal(barrier, inc=1, device_id={axis: me + side * 2**k}, device_id_type=MESH)
    inner = jnp.where(me > 0, 1, 0) + jnp.where(me < count - 1, 1, 0)
    return inner + steps - 1


def step_kernel(nx, ny, cx, cy, cz, fields_hbm, material_ref, permit_ref, out_ref,
                grid_x, grid_y, y_out, y_low, y_high, coef_x,
                gain_x, pivot_x, left_x, right_x, solved_x,
                coef_y, gain_y, pivot_y, left_y, right_y, solved_y,
                load_sem, halo_sems, *line_refs):
    half_step = COURANT / 2.0
    barrier = pltpu.get_barrier_semaphore()
    load = pltpu.make_async_copy(fields_hbm, grid_x.at[:, pl.ds(1, cx)], load_sem)
    load.start()
    waits = greet("gx", nx, barrier) + greet("gy", ny, barrier)
    line_x = Line("gx", nx, line_refs[:9])
    line_y = Line("gy", ny, line_refs[9:])

    x_halo = both_ways("gx", nx, grid_x.at[pl.ds(1, 5), 1], grid_x.at[pl.ds(1, 5), cx],
                       grid_x.at[pl.ds(1, 5), 0], grid_x.at[pl.ds(1, 5), cx + 1], halo_sems.at[0])
    y_halo = both_ways("gy", ny, y_out.at[0], y_out.at[1], y_low, y_high, halo_sems.at[1])
    mid_halo = both_ways("gy", ny, grid_y.at[:, pl.ds(cx, cx)], grid_y.at[:, pl.ds(cx * cy, cx)],
                         grid_y.at[:, pl.ds(0, cx)], grid_y.at[:, pl.ds(cx * (cy + 1), cx)],
                         halo_sems.at[2])
    load.wait()
    for slot, member in enumerate(Y_MEMBERS):
        y_out[0, slot] = jnp.concatenate([grid_x[member, 1 + i, 0:1] for i in range(cx)], axis=0)
        y_out[1, slot] = jnp.concatenate([grid_x[member, 1 + i, cy - 1:cy] for i in range(cx)], axis=0)
    pl.semaphore_wait(barrier, waits)
    x_halo[0]()
    y_halo[0]()

    def coefs(i, carry):
        which = material_ref[i]
        permit = jnp.zeros(which.shape, jnp.float32)
        for entry in range(permit_ref.shape[0]):
            permit = jnp.where(which == entry, permit_ref[entry], permit)
        coef_x[pl.ds(pl.multiple_of(i * cy, 8), cy), :] = (half_step * half_step) / permit
        return carry

    lax.fori_loop(0, cx, coefs, 0)
    coef_plane = lambda i: coef_x[pl.ds(pl.multiple_of(i * cy, 8), cy), :]
    factor(cx, coef_plane, gain_x, pivot_x, left_x, right_x)
    line_x.mat_start(left_x, right_x)

    for j in range(cy):
        coef_y[j] = coef_x[pl.ds(j, cx, stride=cy), :]
    factor(cy, lambda j: coef_y[j], gain_y, pivot_y, left_y, right_y)
    line_y.mat_start(left_y, right_y)

    x_halo[1]()
    y_halo[1]()
    y_slot = {member: slot for slot, member in enumerate(Y_MEMBERS)}

    def forward_x(i, carry):
        centre = [grid_x[m, i + 1] for m in range(6)]
        slope_x = lambda m: 0.5 * (grid_x[m, i + 2] - grid_x[m, i])
        slope_y = lambda m: slope_rows(
            centre[m], y_low[y_slot[m], pl.ds(i, 1), :], y_high[y_slot[m], pl.ds(i, 1), :])
        right = updated(centre, slope_x, slope_y, coef_plane(i) * (1.0 / half_step), half_step)
        gain, pivot = gain_x[i], pivot_x[i]
        now = [right[m] * pivot + gain * carry[m] for m in range(6)]
        for m in range(6):
            solved_x[m, i] = now[m]
        return tuple(now)

    lax.fori_loop(0, cx, forward_x, (jnp.zeros((cy, cz), jnp.float32),) * 6)
    sweep_back(cx, gain_x, solved_x)
    line_x.rhs_start(solved_x)
    for k in range(max(line_x.steps, line_y.steps)):
        if k < line_x.steps:
            line_x.mat_merge(k)
        if k < line_y.steps:
            line_y.mat_merge(k)
    for k in range(line_x.steps):
        for j in range(len(CHUNKS)):
            line_x.rhs_merge(k, j)

    for i in range(cx):
        left, right = left_x[i], right_x[i]
        for m in range(6):
            grid_y[m, pl.ds(cx + i, cy, stride=cx), :] = (
                solved_x[m, i] + left * line_x.ends[0, m] + right * line_x.ends[1, m])
    mid_halo[0]()
    mid_halo[1]()

    y_plane = lambda m, j: grid_y[m, pl.ds(pl.multiple_of(j * cx, 8), cx), :]

    def forward_y(j, carry):
        centre = [y_plane(m, j + 1) for m in range(6)]
        slope_y = lambda m: 0.5 * (y_plane(m, j + 2) - y_plane(m, j))
        slope_x = lambda m: slope_rows(
            centre[m], line_x.ends[0, m, pl.ds(j, 1), :], line_x.ends[1, m, pl.ds(j, 1), :])
        right = updated(centre, slope_x, slope_y, coef_y[j] * (1.0 / half_step), half_step)
        gain, pivot = gain_y[j], pivot_y[j]
        now = [right[m] * pivot + gain * carry[m] for m in range(6)]
        for m in range(6):
            solved_y[m, j] = now[m]
        return tuple(now)

    lax.fori_loop(0, cy, forward_y, (jnp.zeros((cx, cz), jnp.float32),) * 6)
    sweep_back(cy, gain_y, solved_y)
    line_y.rhs_start(solved_y)
    for k in range(line_y.steps):
        for j in range(len(CHUNKS)):
            line_y.rhs_merge(k, j)
    for j in range(cy):
        left, right = left_y[j], right_y[j]
        for m in range(6):
            out_ref[m, pl.ds(j, cx, stride=cy), :] = (
                solved_y[m, j] + left * line_y.ends[0, m] + right * line_y.ends[1, m])
    for halo in (x_halo, y_halo, mid_halo):
        halo[2]()
    line_x.drain()
    line_y.drain()


def line_scratch(count, rows, lanes):
    steps = count.bit_length() - 1
    f32 = jnp.float32
    return [
        pltpu.VMEM((steps, 4, rows, lanes), f32),
        pltpu.VMEM((steps, 4, rows, lanes), f32),
        pltpu.VMEM((steps, 2, 6, rows, lanes), f32),
        pltpu.VMEM((steps, 2, 6, rows, lanes), f32),
        pltpu.VMEM((steps, 7, rows, lanes), f32),
        pltpu.VMEM((4, rows, lanes), f32),
        pltpu.VMEM((2, 6, rows, lanes), f32),
        pltpu.SemaphoreType.DMA((2, steps)),
        pltpu.SemaphoreType.DMA((2, steps, len(CHUNKS))),
    ]


def split_step(nx, ny, fields, material, permittivity):
    _, cx, cy, cz = fields.shape
    f32 = jnp.float32
    x_lines = [pltpu.VMEM((cx, cy, cz), f32)] * 4
    y_lines = [pltpu.VMEM((cy, cx, cz), f32)] * 4
    result = pl.pallas_call(
        functools.partial(step_kernel, nx, ny, cx, cy, cz),
        out_shape=jax.ShapeDtypeStruct((6, cx * cy, cz), f32),
        in_specs=[
            pl.BlockSpec(memory_space=pl.ANY),
            pl.BlockSpec(memory_space=pltpu.VMEM),
            pl.BlockSpec(memory_space=pltpu.SMEM),
        ],
        out_specs=pl.BlockSpec(memory_space=pltpu.VMEM),
        scratch_shapes=[
            pltpu.VMEM((6, cx + 2, cy, cz), f32),
            pltpu.VMEM((6, (cy + 2) * cx, cz), f32),
            pltpu.VMEM((2, 4, cx, cz), f32),
            pltpu.VMEM((4, cx, cz), f32),
            pltpu.VMEM((4, cx, cz), f32),
            pltpu.VMEM((cx * cy, cz), f32),
            *x_lines,
            pltpu.VMEM((6, cx, cy, cz), f32),
            pltpu.VMEM((cy, cx, cz), f32),
            *y_lines,
            pltpu.VMEM((6, cy, cx, cz), f32),
            pltpu.SemaphoreType.DMA,
            pltpu.SemaphoreType.DMA((3, 4)),
            *line_scratch(nx, cy, cz),
            *line_scratch(ny, cx, cz),
        ],
        compiler_params=pltpu.CompilerParams(collective_id=0, has_side_effects=True),
        name="split_step",
    )(fields, material, permittivity)
    return result


def far_kernel(nx, ny, scale, cell_ref, new_ref, cell_col, owner_col, weight_ref, out_ref,
               rows_ref, parts, landed, send_sems, recv_sems):
    count = nx * ny
    me = lax.axis_index("gx") * ny + lax.axis_index("gy")
    barrier = pltpu.get_barrier_semaphore()

    def hello(k, carry):
        to = (me + k) % count
        pl.semaphore_signal(barrier, inc=1, device_id=(to // ny, to % ny), device_id_type=MESH)
        return carry

    lax.fori_loop(1, count, hello, 0)
    patches = cell_ref.shape[0]
    lanes = new_ref.shape[2]

    def fetch(q, carry):
        for u in range(8):
            p = q * 8 + u
            row = cell_ref[p] // lanes
            for m in range(6):
                rows_ref[m, pl.ds(p, 1), :] = new_ref[m, pl.ds(row, 1), :]
        return carry

    lax.fori_loop(0, patches // 8, fetch, 0)
    at = lax.broadcasted_iota(jnp.int32, (patches, lanes), 1)
    hit = at == (cell_col[...] & (lanes - 1))
    hot = (lax.broadcasted_iota(jnp.int32, (patches, count), 1) == owner_col[...]).astype(jnp.float32)
    angles = out_ref.shape[1]
    for m in range(6):
        value = jnp.sum(jnp.where(hit, rows_ref[m], 0.0), axis=1, keepdims=True)
        product = lax.dot_general(hot * value, weight_ref[...], (((0,), (0,)), ((), ())),
                                  precision=lax.Precision.HIGHEST,
                                  preferred_element_type=jnp.float32)
        for s in range(2):
            parts[pl.ds(s * 6 + m, count, stride=16), :] = product[:, s * angles:(s + 1) * angles]
    pl.semaphore_wait(barrier, count - 1)

    def piece(k):
        to = (me + k) % count
        return pltpu.make_async_remote_copy(
            parts.at[pl.ds(pl.multiple_of(to * 16, 16), 16)], landed.at[k],
            send_sems.at[k], recv_sems.at[k],
            device_id=(to // ny, to % ny), device_id_type=MESH)

    def send(k, carry):
        piece(k).start()
        return carry

    lax.fori_loop(1, count, send, 0)

    def add(k, total):
        piece(k).wait_recv()
        return total + landed[k]

    total = lax.fori_loop(1, count, add, parts[pl.ds(pl.multiple_of(me * 16, 16), 16), :])
    out_ref[...] = total[:12] * scale

    def done(k, carry):
        piece(k).wait_send()
        return carry

    lax.fori_loop(1, count, done, 0)


def far_sums(nx, ny, scale, new_flat, patch_cell, patch_owner, weights):
    count = nx * ny
    patches = patch_cell.shape[0]
    lanes = new_flat.shape[2]
    vmem = pl.BlockSpec(memory_space=pltpu.VMEM)
    return pl.pallas_call(
        functools.partial(far_kernel, nx, ny, scale),
        out_shape=jax.ShapeDtypeStruct((12, ANG_DEV), jnp.float32),
        in_specs=[pl.BlockSpec(memory_space=pltpu.SMEM), vmem, vmem, vmem, vmem],
        out_specs=vmem,
        scratch_shapes=[
            pltpu.VMEM((6, patches, lanes), jnp.float32),
            pltpu.VMEM((count * 16, ANG_DEV), jnp.float32),
            pltpu.VMEM((count, 16, ANG_DEV), jnp.float32),
            pltpu.SemaphoreType.DMA((count,)),
            pltpu.SemaphoreType.DMA((count,)),
        ],
        compiler_params=pltpu.CompilerParams(collective_id=1, has_side_effects=True),
        name="far_sums",
    )(patch_cell, new_flat, patch_cell[:, None], patch_owner, weights)


def far_phase(pos_x, pos_y, pos_z, owner_f, owners, angle_count):
    theta = math.pi * (jnp.arange(angle_count, dtype=jnp.float32) + 0.5) / angle_count
    azimuth = owner_f * (2.0 * math.pi / owners)
    sin_theta = jnp.sin(theta)[None, :]
    cos_theta = jnp.cos(theta)[None, :]
    cos_phi = jnp.cos(azimuth)[:, None]
    sin_phi = jnp.sin(azimuth)[:, None]
    return KAPPA * (
        pos_x[:, None] * sin_theta * cos_phi
        + pos_y[:, None] * sin_theta * sin_phi
        + pos_z[:, None] * cos_theta
    )


def local(nx, ny, fields, material, permittivity, patch_cell, patch_owner):
    _, cells_x, cells_y, cells_z = fields.shape
    grid_x = (lax.axis_index("gx") * cells_x + patch_cell // (cells_y * cells_z)).astype(jnp.float32)
    grid_y = (lax.axis_index("gy") * cells_y + patch_cell // cells_z % cells_y).astype(jnp.float32)
    grid_z = (patch_cell % cells_z).astype(jnp.float32)
    owner = patch_owner[:, 0].astype(jnp.float32)
    phases = far_phase(grid_x, grid_y, grid_z, owner, nx * ny, ANG_DEV)
    weights = jnp.concatenate([jnp.cos(phases), jnp.sin(phases)], axis=1)
    new_flat = split_step(nx, ny, fields, material, permittivity)
    scale = 1.0 / math.sqrt(patch_cell.shape[0])
    far_field = far_sums(nx, ny, scale, new_flat, patch_cell, patch_owner, weights)
    return new_flat.reshape(fields.shape), far_field


def solution(mesh):
    return jax.shard_map(
        functools.partial(local, mesh.shape["gx"], mesh.shape["gy"]),
        mesh=mesh,
        in_specs=(
            P(None, "gx", "gy", None),
            P("gx", "gy", None),
            P(),
            P(("gx", "gy")),
            P(("gx", "gy"), None),
        ),
        out_specs=(P(None, "gx", "gy", None), P(None, ("gx", "gy"))),
        check_vma=False,
    )
```

profile of v0, /device:TPU:0, one launch (start us, length us, event | category | flops | bytes accessed | tf_op | source)
XLA Modules:
  0.0 59.2 jit_solution(10941897831097638850)
XLA Ops:
  0.7 0.7 %add_convert_fusion = (f32[256]{0:T(256)S(1)}, f32[256]{0:T(256)S(1)}, f32[256]{0:T(256)S(1)}) fusion(s32[256]{0:T(256)} %cell_ref.1, s32[]{:T(128)S(6)} %mul.81, s32[]{:T(128)S(6)} %mul.90), kind=kLoop, calls=%fused_computation.15 | loop fusion | flops 9216 | bytes 4104 | tf_op jit(solution)/shard_map/convert_element_type | solution.py:526
  1.4 0.7 %fusion.6 = (f32[256,1]{0,1:T(1,128)S(1)}, f32[256,1]{0,1:T(1,128)S(1)}) fusion(s32[256,1]{0,1:T(1,128)} %param.9), kind=kLoop, calls=%fused_computation.18 | loop fusion | flops 512 | bytes 3072 | tf_op jit(solution)/shard_map/cos | solution.py:515
  2.1 1.5 %copy.8.cell_col = s32[256,1]{1,0:T(8,128)} copy(s32[256,1]{0,1:T(1,128)} %bitcast.5) | data formatting | bytes 2048 | tf_op jit(solution)/shard_map/broadcast_in_dim | solution.py:507
  3.6 1.5 %copy.9.owner_col = s32[256,1]{1,0:T(8,128)} copy(s32[256,1]{0,1:T(1,128)} %param.9) | data formatting | bytes 2048 | tf_op args[4]
  5.1 0.6 fusion.1
  5.6 0.7 %pad_maximum_fusion.weight_ref = f32[256,256]{1,0:T(8,128)} fusion(f32[256,128]{1,0:T(8,128)S(1)} %get-tuple-element.3, f32[256,128]{1,0:T(8,128)S(1)} %get-tuple-element.2), kind=kLoop, calls=%fused_computation | loop fusion | flops 65536 | bytes 524288 | tf_op jit(solution)/shard_map/concatenate | solution.py:531
  6.4 36.2 %split_step.1.new_ref = f32[6,384,128]{2,1,0:T(8,128)} custom-call(f32[6,16,24,128]{3,2,1,0:T(8,128)} %fields_hbm.1, s32[16,24,128]{2,1,0:T(8,128)} %material_ref.1, f32[16]{0:T(128)} %permit_ref.1), custom_call_target="tpu_custom_call" | custom-call | tf_op jit(solution)/shard_map/split_step/pallas_call | solution.py:392
  42.6 0.0 copy-start
  42.6 15.0 %far_sums.1 = f32[12,128]{1,0:T(8,128)} custom-call(s32[256]{0:T(256)} %cell_ref.1, f32[6,384,128]{2,1,0:T(8,128)} %split_step.1.new_ref, s32[256,1]{1,0:T(8,128)} %copy.8.cell_col, s32[256,1]{1,0:T(8,128)} %copy.9.owner_col, f32[256,256]{1,0:T(8,128)} %pad_maximum_fusion.weight_ref), custom_call_target="tpu_custom_call" | custom-call | tf_op jit(solution)/shard_map/far_sums/pallas_call | solution.py:493
  57.6 0.0 copy-done
  57.6 0.0 copy-start.1
  57.6 1.0 %copy.12 = f32[6,16,24,128]{3,2,1,0:T(8,128)} copy(f32[6,16,24,128]{3,2,1,0:T(8,128)S(1)} %bitcast.4) | data formatting | bytes 2359296
  58.6 0.0 copy-done.1
  58.6 0.6 %copy.13 = f32[12,128]{1,0:T(8,128)} copy(f32[12,128]{1,0:T(8,128)S(1)} %copy-done.1) | data formatting | bytes 12288
  (1 shorter events, 0.0 us)
Async XLA Ops:
  42.6 15.0 %copy-start = (f32[6,384,128]{2,1,0:T(8,128)S(1)}, f32[6,384,128]{2,1,0:T(8,128)}, u32[]{:S(2)}) copy-start(f32[6,384,128]{2,1,0:T(8,128)} %split_step.1.new_ref) | copy-start | bytes 3538948
  57.6 1.0 %copy-start.1 = (f32[12,128]{1,0:T(8,128)S(1)}, f32[12,128]{1,0:T(8,128)}, u32[]{:S(2)}) copy-start(f32[12,128]{1,0:T(8,128)} %far_sums.1) | copy-start | bytes 18436
where the time goes:
time: 59.5 us; the launch traced here: 59.2 us
  Pallas kernels  51.2 us (86%)
  local copies, waits for them, and re-layouts  4.55 us (8%)
  other arithmetic  2.78 us (5%)
  between operations  0.69 us (1%)
    pallas_call x1, Pallas kernels, split_step(): pl.pallas_call(functools.partial(step_kernel, nx, ny, cx, cy, cz), out_sh...  36.2 us
    pallas_call x1, Pallas kernels, far_sums(): pl.pallas_call(functools.partial(far_kernel, nx, ny, scale), out_shape=ja...  15 us
    unnamed x7, local copies, waits for them, and re-layouts  3.09 us
    broadcast_in_dim x1, local copies, waits for them, and re-layouts, far_sums(): patch_cell[:, None]  1.46 us

commit v1 on v0

--- a/solution.py
+++ b/solution.py
@@ -55,7 +55,7 @@
         left_ref[i] = left
         return gain, left
 
-    lax.fori_loop(0, length, forward, (zero, jnp.ones_like(zero)))
+    lax.fori_loop(0, length, forward, (zero, jnp.ones_like(zero)), unroll=2)
 
     def backward(k, carry):
         left_next, right_next = carry
@@ -67,7 +67,7 @@
         right_ref[i] = right
         return left, right
 
-    lax.fori_loop(0, length, backward, (zero, jnp.ones_like(zero)))
+    lax.fori_loop(0, length, backward, (zero, jnp.ones_like(zero)), unroll=4)
 
 
 def sweep_back(length, gain_ref, solved_ref):
@@ -80,7 +80,7 @@
         return tuple(now)
 
     zero = jnp.zeros(gain_ref.shape[1:], jnp.float32)
-    lax.fori_loop(0, length, backward, (zero,) * 6)
+    lax.fori_loop(0, length, backward, (zero,) * 6, unroll=4)
 
 
 class Line:
@@ -237,35 +237,75 @@
     return start, wait, drain
 
 
-def greet(axis, count, barrier):
-    me = lax.axis_index(axis)
-
-    @pl.when(me > 0)
-    def _():
-        pl.semaphore_signal(barrier, inc=1, device_id={axis: me - 1}, device_id_type=MESH)
-
-    @pl.when(me < count - 1)
-    def _():
-        pl.semaphore_signal(barrier, inc=1, device_id={axis: me + 1}, device_id_type=MESH)
-
-    steps = count.bit_length() - 1
-    for k in range(1, steps):
-        side = 1 - 2 * ((me // 2**k) % 2)
-        pl.semaphore_signal(barrier, inc=1, device_id={axis: me + side * 2**k}, device_id_type=MESH)
-    inner = jnp.where(me > 0, 1, 0) + jnp.where(me < count - 1, 1, 0)
-    return inner + steps - 1
-
-
-def step_kernel(nx, ny, cx, cy, cz, fields_hbm, material_ref, permit_ref, out_ref,
+def greet_all(count, ny, me, barrier):
+    def hello(k, carry):
+        to = (me + k) % count
+        pl.semaphore_signal(barrier, inc=1, device_id=(to // ny, to % ny), device_id_type=MESH)
+        return carry
+
+    lax.fori_loop(1, count, hello, 0)
+
+
+def cos_sin(angle):
+    turns = jnp.floor(angle * (2.0 / math.pi) + 0.5)
+    rest = ((angle - turns * 1.5703125) - turns * 4.837512969970703125e-4) - turns * 7.54978995489188216e-8
+    square = rest * rest
+    sine = ((-1.9515295891e-4 * square + 8.3321608736e-3) * square - 1.6666654611e-1) * square * rest + rest
+    cosine = (
+        (2.443315711809948e-5 * square - 1.388731625493765e-3) * square + 4.166664568298827e-2
+    ) * square * square - 0.5 * square + 1.0
+    quarter = turns.astype(jnp.int32) & 3
+    swap = (quarter & 1) == 1
+    plain_cos = jnp.where(swap, sine, cosine)
+    plain_sin = jnp.where(swap, cosine, sine)
+    minus_cos = (quarter == 1) | (quarter == 2)
+    return jnp.where(minus_cos, -plain_cos, plain_cos), jnp.where(quarter >= 2, -plain_sin, plain_sin)
+
+
+def fill_weights(count, cx, cy, cz, cell_row, owner_row, weight_ref):
+    angles = weight_ref.shape[0] // 2
+    cell = cell_row[...]
+    bits = cz.bit_length() - 1
+    line = lax.shift_right_logical(cell, jnp.full_like(cell, bits))
+    at_x = jnp.zeros_like(cell)
+    for i in range(1, cx):
+        at_x = at_x + jnp.where(line >= i * cy, 1, 0)
+    at_y = line - at_x * cy
+    pos_x = (at_x + lax.axis_index("gx") * cx).astype(jnp.float32)
+    pos_y = (at_y + lax.axis_index("gy") * cy).astype(jnp.float32)
+    pos_z = (cell - line * cz).astype(jnp.float32)
+    cos_phi, sin_phi = cos_sin(owner_row[...].astype(jnp.float32) * (2.0 * math.pi / count))
+    shape = (8, cell.shape[1])
+    wide = [jnp.broadcast_to(v, shape) for v in (pos_x, pos_y, pos_z, cos_phi, sin_phi)]
+
+    def group(g, carry):
+        pos_x, pos_y, pos_z, cos_phi, sin_phi = carry
+        start = pl.multiple_of(g * 8, 8)
+        index = (lax.broadcasted_iota(jnp.int32, shape, 0) + start).astype(jnp.float32)
+        cos_theta, sin_theta = cos_sin(math.pi * (index + 0.5) / angles)
+        phase = KAPPA * (pos_x * sin_theta * cos_phi + pos_y * sin_theta * sin_phi + pos_z * cos_theta)
+        cosine, sine = cos_sin(phase)
+        weight_ref[pl.ds(start, 8), :] = cosine
+        weight_ref[pl.ds(start + angles, 8), :] = sine
+        return carry
+
+    lax.fori_loop(0, angles // 8, group, tuple(wide))
+
+
+def step_kernel(nx, ny, cx, cy, cz, scale, fields_hbm, material_ref, permit_ref, cell_smem,
+                cell_row, owner_row, out_ref, far_ref,
                 grid_x, grid_y, y_out, y_low, y_high, coef_x,
                 gain_x, pivot_x, left_x, right_x, solved_x,
                 coef_y, gain_y, pivot_y, left_y, right_y, solved_y,
-                load_sem, halo_sems, *line_refs):
+                weight_ref, packed, samples, spread, parts, landed,
+                load_sem, halo_sems, part_sems, *line_refs):
     half_step = COURANT / 2.0
+    count = nx * ny
+    me = lax.axis_index("gx") * ny + lax.axis_index("gy")
     barrier = pltpu.get_barrier_semaphore()
     load = pltpu.make_async_copy(fields_hbm, grid_x.at[:, pl.ds(1, cx)], load_sem)
     load.start()
-    waits = greet("gx", nx, barrier) + greet("gy", ny, barrier)
+    greet_all(count, ny, me, barrier)
     line_x = Line("gx", nx, line_refs[:9])
     line_y = Line("gy", ny, line_refs[9:])
 
@@ -275,13 +315,6 @@
     mid_halo = both_ways("gy", ny, grid_y.at[:, pl.ds(cx, cx)], grid_y.at[:, pl.ds(cx * cy, cx)],
                          grid_y.at[:, pl.ds(0, cx)], grid_y.at[:, pl.ds(cx * (cy + 1), cx)],
                          halo_sems.at[2])
-    load.wait()
-    for slot, member in enumerate(Y_MEMBERS):
-        y_out[0, slot] = jnp.concatenate([grid_x[member, 1 + i, 0:1] for i in range(cx)], axis=0)
-        y_out[1, slot] = jnp.concatenate([grid_x[member, 1 + i, cy - 1:cy] for i in range(cx)], axis=0)
-    pl.semaphore_wait(barrier, waits)
-    x_halo[0]()
-    y_halo[0]()
 
     def coefs(i, carry):
         which = material_ref[i]
@@ -291,16 +324,19 @@
         coef_x[pl.ds(pl.multiple_of(i * cy, 8), cy), :] = (half_step * half_step) / permit
         return carry
 
-    lax.fori_loop(0, cx, coefs, 0)
+    lax.fori_loop(0, cx, coefs, 0, unroll=2)
+    load.wait()
+    for slot, member in enumerate(Y_MEMBERS):
+        y_out[0, slot] = jnp.concatenate([grid_x[member, 1 + i, 0:1] for i in range(cx)], axis=0)
+        y_out[1, slot] = jnp.concatenate([grid_x[member, 1 + i, cy - 1:cy] for i in range(cx)], axis=0)
+    pl.semaphore_wait(barrier, count - 1)
+    x_halo[0]()
+    y_halo[0]()
     coef_plane = lambda i: coef_x[pl.ds(pl.multiple_of(i * cy, 8), cy), :]
     factor(cx, coef_plane, gain_x, pivot_x, left_x, right_x)
     line_x.mat_start(left_x, right_x)
-
     for j in range(cy):
         coef_y[j] = coef_x[pl.ds(j, cx, stride=cy), :]
-    factor(cy, lambda j: coef_y[j], gain_y, pivot_y, left_y, right_y)
-    line_y.mat_start(left_y, right_y)
-
     x_halo[1]()
     y_halo[1]()
     y_slot = {member: slot for slot, member in enumerate(Y_MEMBERS)}
@@ -318,16 +354,23 @@
         return tuple(now)
 
     lax.fori_loop(0, cx, forward_x, (jnp.zeros((cy, cz), jnp.float32),) * 6)
+    early = min(2, line_x.steps)
+    line_x.mat_merge(0)
     sweep_back(cx, gain_x, solved_x)
     line_x.rhs_start(solved_x)
-    for k in range(max(line_x.steps, line_y.steps)):
-        if k < line_x.steps:
+    if early > 1:
+        line_x.mat_merge(1)
+    factor(cy, lambda j: coef_y[j], gain_y, pivot_y, left_y, right_y)
+    line_y.mat_start(left_y, right_y)
+    for k in range(line_x.steps):
+        if k >= early:
             line_x.mat_merge(k)
+        for j in range(len(CHUNKS)):
+            line_x.rhs_merge(k, j)
         if k < line_y.steps:
             line_y.mat_merge(k)
-    for k in range(line_x.steps):
-        for j in range(len(CHUNKS)):
-            line_x.rhs_merge(k, j)
+    for k in range(line_x.steps, line_y.steps):
+        line_y.mat_merge(k)
 
     for i in range(cx):
         left, right = left_x[i], right_x[i]
@@ -335,6 +378,7 @@
             grid_y[m, pl.ds(cx + i, cy, stride=cx), :] = (
                 solved_x[m, i] + left * line_x.ends[0, m] + right * line_x.ends[1, m])
     mid_halo[0]()
+    fill_weights(count, cx, cy, cz, cell_row, owner_row, weight_ref)
     mid_halo[1]()
 
     y_plane = lambda m, j: grid_y[m, pl.ds(pl.multiple_of(j * cx, 8), cx), :]
@@ -351,7 +395,7 @@
             solved_y[m, j] = now[m]
         return tuple(now)
 
-    lax.fori_loop(0, cy, forward_y, (jnp.zeros((cx, cz), jnp.float32),) * 6)
+    lax.fori_loop(0, cy, forward_y, (jnp.zeros((cx, cz), jnp.float32),) * 6, unroll=2)
     sweep_back(cy, gain_y, solved_y)
     line_y.rhs_start(solved_y)
     for k in range(line_y.steps):
@@ -360,12 +404,69 @@
     for j in range(cy):
         left, right = left_y[j], right_y[j]
         for m in range(6):
-            out_ref[m, pl.ds(j, cx, stride=cy), :] = (
-                solved_y[m, j] + left * line_y.ends[0, m] + right * line_y.ends[1, m])
+            value = solved_y[m, j] + left * line_y.ends[0, m] + right * line_y.ends[1, m]
+            out_ref[m, pl.ds(j, cx, stride=cy), :] = value
+            packed[pl.ds(j * 8 + m, cx, stride=cy * 8), :] = value
+
+    patches = cell_smem.shape[0]
+
+    def fetch(q, carry):
+        for u in range(8):
+            p = q * 8 + u
+            line = cell_smem[p] // cz
+            samples[pl.ds(p, 8, stride=patches), :] = packed[pl.ds(line * 8, 8), :]
+        return carry
+
+    lax.fori_loop(0, patches // 8, fetch, 0)
+    spot = jnp.transpose(jnp.broadcast_to(cell_row[...] & (cz - 1), (cz, patches)))
+    hit = lax.broadcasted_iota(jnp.int32, (patches, cz), 1) == spot
+    column = lax.broadcasted_iota(jnp.int32, (patches, 128), 1)
+    table = jnp.zeros((patches, 128), jnp.float32)
+    for m in range(6):
+        value = jnp.sum(jnp.where(hit, samples[pl.ds(m * patches, patches), :], 0.0), axis=1, keepdims=True)
+        table = jnp.where(column == m, value, table)
+    values = jnp.transpose(table)
+    owner = owner_row[...]
+    hot = (lax.broadcasted_iota(jnp.int32, (count, patches), 0) == owner).astype(jnp.float32)
+    for m in range(6):
+        spread[pl.ds(m * count, count), :] = hot * values[m:m + 1]
+    product = lax.dot_general(spread[...], weight_ref[...], (((1,), (1,)), ((), ())),
+                              precision=lax.Precision.HIGHEST, preferred_element_type=jnp.float32)
+    angles = far_ref.shape[1]
+    for m in range(6):
+        for s in range(2):
+            parts[pl.ds(s * 6 + m, count, stride=16), :] = (
+                product[m * count:(m + 1) * count, s * angles:(s + 1) * angles])
+
+    def piece(k):
+        to = (me + k) % count
+        return pltpu.make_async_remote_copy(
+            parts.at[pl.ds(pl.multiple_of(to * 16, 16), 16)], landed.at[k],
+            part_sems.at[0, k], part_sems.at[1, k],
+            device_id=(to // ny, to % ny), device_id_type=MESH)
+
+    def send(k, carry):
+        piece(k).start()
+        return carry
+
+    lax.fori_loop(1, count, send, 0)
     for halo in (x_halo, y_halo, mid_halo):
         halo[2]()
     line_x.drain()
     line_y.drain()
+
+    def add(k, total):
+        piece(k).wait_recv()
+        return total + landed[k]
+
+    total = lax.fori_loop(1, count, add, parts[pl.ds(pl.multiple_of(me * 16, 16), 16), :])
+    far_ref[...] = total[:12] * scale
+
+    def done(k, carry):
+        piece(k).wait_send()
+        return carry
+
+    lax.fori_loop(1, count, done, 0)
 
 
 def line_scratch(count, rows, lanes):
@@ -384,20 +485,23 @@
     ]
 
 
-def split_step(nx, ny, fields, material, permittivity):
+def local(nx, ny, fields, material, permittivity, patch_cell, patch_owner):
     _, cx, cy, cz = fields.shape
     f32 = jnp.float32
+    count = nx * ny
+    patches = patch_cell.shape[0]
+    vmem = pl.BlockSpec(memory_space=pltpu.VMEM)
+    smem = pl.BlockSpec(memory_space=pltpu.SMEM)
     x_lines = [pltpu.VMEM((cx, cy, cz), f32)] * 4
     y_lines = [pltpu.VMEM((cy, cx, cz), f32)] * 4
-    result = pl.pallas_call(
-        functools.partial(step_kernel, nx, ny, cx, cy, cz),
-        out_shape=jax.ShapeDtypeStruct((6, cx * cy, cz), f32),
-        in_specs=[
-            pl.BlockSpec(memory_space=pl.ANY),
-            pl.BlockSpec(memory_space=pltpu.VMEM),
-            pl.BlockSpec(memory_space=pltpu.SMEM),
-        ],
-        out_specs=pl.BlockSpec(memory_space=pltpu.VMEM),
+    new_flat, far_field = pl.pallas_call(
+        functools.partial(step_kernel, nx, ny, cx, cy, cz, 1.0 / math.sqrt(patches)),
+        out_shape=(
+            jax.ShapeDtypeStruct((6, cx * cy, cz), f32),
+            jax.ShapeDtypeStruct((12, ANG_DEV), f32),
+        ),
+        in_specs=[pl.BlockSpec(memory_space=pltpu.HBM), vmem, smem, smem, vmem, vmem],
+        out_specs=(vmem, vmem),
         scratch_shapes=[
             pltpu.VMEM((6, cx + 2, cy, cz), f32),
             pltpu.VMEM((6, (cy + 2) * cx, cz), f32),
@@ -410,128 +514,22 @@
             pltpu.VMEM((cy, cx, cz), f32),
             *y_lines,
             pltpu.VMEM((6, cy, cx, cz), f32),
+            pltpu.VMEM((2 * ANG_DEV, patches), f32),
+            pltpu.VMEM((cx * cy * 8, cz), f32),
+            pltpu.VMEM((8 * patches, cz), f32),
+            pltpu.VMEM((6 * count, patches), f32),
+            pltpu.VMEM((count * 16, ANG_DEV), f32),
+            pltpu.VMEM((count, 16, ANG_DEV), f32),
             pltpu.SemaphoreType.DMA,
             pltpu.SemaphoreType.DMA((3, 4)),
+            pltpu.SemaphoreType.DMA((2, count)),
             *line_scratch(nx, cy, cz),
             *line_scratch(ny, cx, cz),
         ],
-        compiler_params=pltpu.CompilerParams(collective_id=0, has_side_effects=True),
+        compiler_params=pltpu.CompilerParams(
+            collective_id=0, has_side_effects=True, vmem_limit_bytes=40 * 2**20),
         name="split_step",
-    )(fields, material, permittivity)
-    return result
-
-
-def far_kernel(nx, ny, scale, cell_ref, new_ref, cell_col, owner_col, weight_ref, out_ref,
-               rows_ref, parts, landed, send_sems, recv_sems):
-    count = nx * ny
-    me = lax.axis_index("gx") * ny + lax.axis_index("gy")
-    barrier = pltpu.get_barrier_semaphore()
-
-    def hello(k, carry):
-        to = (me + k) % count
-        pl.semaphore_signal(barrier, inc=1, device_id=(to // ny, to % ny), device_id_type=MESH)
-        return carry
-
-    lax.fori_loop(1, count, hello, 0)
-    patches = cell_ref.shape[0]
-    lanes = new_ref.shape[2]
-
-    def fetch(q, carry):
-        for u in range(8):
-            p = q * 8 + u
-            row = cell_ref[p] // lanes
-            for m in range(6):
-                rows_ref[m, pl.ds(p, 1), :] = new_ref[m, pl.ds(row, 1), :]
-        return carry
-
-    lax.fori_loop(0, patches // 8, fetch, 0)
-    at = lax.broadcasted_iota(jnp.int32, (patches, lanes), 1)
-    hit = at == (cell_col[...] & (lanes - 1))
-    hot = (lax.broadcasted_iota(jnp.int32, (patches, count), 1) == owner_col[...]).astype(jnp.float32)
-    angles = out_ref.shape[1]
-    for m in range(6):
-        value = jnp.sum(jnp.where(hit, rows_ref[m], 0.0), axis=1, keepdims=True)
-        product = lax.dot_general(hot * value, weight_ref[...], (((0,), (0,)), ((), ())),
-                                  precision=lax.Precision.HIGHEST,
-                                  preferred_element_type=jnp.float32)
-        for s in range(2):
-            parts[pl.ds(s * 6 + m, count, stride=16), :] = product[:, s * angles:(s + 1) * angles]
-    pl.semaphore_wait(barrier, count - 1)
-
-    def piece(k):
-        to = (me + k) % count
-        return pltpu.make_async_remote_copy(
-            parts.at[pl.ds(pl.multiple_of(to * 16, 16), 16)], landed.at[k],
-            send_sems.at[k], recv_sems.at[k],
-            device_id=(to // ny, to % ny), device_id_type=MESH)
-
-    def send(k, carry):
-        piece(k).start()
-        return carry
-
-    lax.fori_loop(1, count, send, 0)
-
-    def add(k, total):
-        piece(k).wait_recv()
-        return total + landed[k]
-
-    total = lax.fori_loop(1, count, add, parts[pl.ds(pl.multiple_of(me * 16, 16), 16), :])
-    out_ref[...] = total[:12] * scale
-
-    def done(k, carry):
-        piece(k).wait_send()
-        return carry
-
-    lax.fori_loop(1, count, done, 0)
-
-
-def far_sums(nx, ny, scale, new_flat, patch_cell, patch_owner, weights):
-    count = nx * ny
-    patches = patch_cell.shape[0]
-    lanes = new_flat.shape[2]
-    vmem = pl.BlockSpec(memory_space=pltpu.VMEM)
-    return pl.pallas_call(
-        functools.partial(far_kernel, nx, ny, scale),
-        out_shape=jax.ShapeDtypeStruct((12, ANG_DEV), jnp.float32),
-        in_specs=[pl.BlockSpec(memory_space=pltpu.SMEM), vmem, vmem, vmem, vmem],
-        out_specs=vmem,
-        scratch_shapes=[
-            pltpu.VMEM((6, patches, lanes), jnp.float32),
-            pltpu.VMEM((count * 16, ANG_DEV), jnp.float32),
-            pltpu.VMEM((count, 16, ANG_DEV), jnp.float32),
-            pltpu.SemaphoreType.DMA((count,)),
-            pltpu.SemaphoreType.DMA((count,)),
-        ],
-        compiler_params=pltpu.CompilerParams(collective_id=1, has_side_effects=True),
-        name="far_sums",
-    )(patch_cell, new_flat, patch_cell[:, None], patch_owner, weights)
-
-
-def far_phase(pos_x, pos_y, pos_z, owner_f, owners, angle_count):
-    theta = math.pi * (jnp.arange(angle_count, dtype=jnp.float32) + 0.5) / angle_count
-    azimuth = owner_f * (2.0 * math.pi / owners)
-    sin_theta = jnp.sin(theta)[None, :]
-    cos_theta = jnp.cos(theta)[None, :]
-    cos_phi = jnp.cos(azimuth)[:, None]
-    sin_phi = jnp.sin(azimuth)[:, None]
-    return KAPPA * (
-        pos_x[:, None] * sin_theta * cos_phi
-        + pos_y[:, None] * sin_theta * sin_phi
-        + pos_z[:, None] * cos_theta
-    )
-
-
-def local(nx, ny, fields, material, permittivity, patch_cell, patch_owner):
-    _, cells_x, cells_y, cells_z = fields.shape
-    grid_x = (lax.axis_index("gx") * cells_x + patch_cell // (cells_y * cells_z)).astype(jnp.float32)
-    grid_y = (lax.axis_index("gy") * cells_y + patch_cell // cells_z % cells_y).astype(jnp.float32)
-    grid_z = (patch_cell % cells_z).astype(jnp.float32)
-    owner = patch_owner[:, 0].astype(jnp.float32)
-    phases = far_phase(grid_x, grid_y, grid_z, owner, nx * ny, ANG_DEV)
-    weights = jnp.concatenate([jnp.cos(phases), jnp.sin(phases)], axis=1)
-    new_flat = split_step(nx, ny, fields, material, permittivity)
-    scale = 1.0 / math.sqrt(patch_cell.shape[0])
-    far_field = far_sums(nx, ny, scale, new_flat, patch_cell, patch_owner, weights)
+    )(fields, material, permittivity, patch_cell, patch_cell[None, :], patch_owner.reshape(1, patches))
     return new_flat.reshape(fields.shape), far_field
 
 

time: 59.5 us -> 50.9 us (0.86)
  Pallas kernels: 51.2 us -> 44.2 us
  other arithmetic: 2.78 us -> 0 us
  local copies, waits for them, and re-layouts: 4.55 us -> 5.82 us
    pallas_call x2 -> x1, Pallas kernels: 51.2 us -> 44.2 us  [local(): pl.pallas_call(functools.partial(step_kernel, nx, ny, cx, cy, cz, 1.0 / m...]
    unnamed x7 -> x12, local copies, waits for them, and re-layouts: 3.09 us -> 5.82 us
    broadcast_in_dim x1 -> x0, local copies, waits for them, and re-layouts: 1.46 us -> none  [far_sums(): patch_cell[:, None]]
    cos x3 -> x0, other arithmetic: 1.35 us -> none  [the longest x1 0.73 us: far_phase(): cos_phi = jnp.cos(azimuth)[:, None]]
    concatenate x1 -> x0, other arithmetic: 0.72 us -> none  [local(): weights = jnp.concatenate([jnp.cos(phases), jnp.sin(phases)], axis=1)]
    convert_element_type x1 -> x0, other arithmetic: 0.71 us -> none  [local(): (lax.axis_index('gx') * cells_x + patch_cell // (cells_y * cells_z)).asty...]
where the time goes in v1:
time: 50.9 us; the launch traced here: 50.7 us
  Pallas kernels  44.2 us (87%)
  local copies, waits for them, and re-layouts  5.82 us (11%)
  between operations  0.65 us (1%)
    pallas_call x1, Pallas kernels, local(): pl.pallas_call(functools.partial(step_kernel, nx, ny, cx, cy, cz, 1.0 / m...  44.2 us
    unnamed x12, local copies, waits for them, and re-layouts  5.82 us

profile of v1, /device:TPU:0, one launch (start us, length us, event | category | flops | bytes accessed | tf_op | source)
XLA Modules:
  0.0 50.7 jit_solution(14134457858843118565)
XLA Ops:
  0.6 0.0 copy-start
  0.6 1.3 %copy-done = f32[6,16,24,128]{3,2,1,0:T(8,128)S(1)} copy-done((f32[6,16,24,128]{3,2,1,0:T(8,128)S(1)}, f32[6,16,24,128]{3,2,1,0:T(8,128)}, u32[]{:S(2)}) %copy-start) | copy-done | bytes 1179672
  1.9 0.0 copy-start.1
  1.9 0.9 %copy-done.1 = s32[16,24,128]{2,1,0:T(8,128)S(1)} copy-done((s32[16,24,128]{2,1,0:T(8,128)S(1)}, s32[16,24,128]{2,1,0:T(8,128)}, u32[]{:S(2)}) %copy-start.1) | copy-done | bytes 196632
  2.8 0.0 copy-start.2
  2.8 0.7 %copy-done.2 = s32[256]{0:T(256)S(1)} copy-done((s32[256]{0:T(256)S(1)}, s32[256]{0:T(256)}, u32[]{:S(2)}) %copy-start.2) | copy-done | bytes 1048
  3.5 0.0 copy-start.3
  3.5 0.7 %copy-done.3 = s32[256,1]{0,1:T(1,128)S(1)} copy-done((s32[256,1]{0,1:T(1,128)S(1)}, s32[256,1]{0,1:T(1,128)}, u32[]{:S(2)}) %copy-start.3) | copy-done | bytes 1048
  4.2 0.0 copy-start.4
  4.2 0.7 %copy-done.4 = f32[16]{0:T(128)S(1)} copy-done((f32[16]{0:T(128)S(1)}, f32[16]{0:T(128)}, u32[]{:S(2)}) %copy-start.4) | copy-done | bytes 88
  4.8 44.2 %split_step.1 = (f32[6,384,128]{2,1,0:T(8,128)S(1)}, f32[12,128]{1,0:T(8,128)S(1)}) custom-call(f32[6,16,24,128]{3,2,1,0:T(8,128)S(1)} %copy-done, s32[16,24,128]{2,1,0:T(8,128)S(1)} %copy-done.1, f32[16]{0:T(128)S(1)} %copy-done.4, s32[256]{0:T(256)S(1)} %copy-done.2, s32[1,256]{1,0:T(1,128)S(1)} %bitcast.4, s32[1,256]{1,0:T(1,128)S(1)} %bitcast.5), custom_call_target="tpu_custom_call" | custom-call | tf_op jit(solution)/shard_map/split_step/pallas_call | solution.py:497
  49.1 1.0 %copy.9 = f32[6,16,24,128]{3,2,1,0:T(8,128)} copy(f32[6,16,24,128]{3,2,1,0:T(8,128)S(1)} %bitcast.3) | data formatting | bytes 2359296
  50.1 0.6 %copy.10 = f32[12,128]{1,0:T(8,128)} copy(f32[12,128]{1,0:T(8,128)S(1)} %get-tuple-element.9) | data formatting | bytes 12288
Async XLA Ops:
  0.6 1.3 %copy-start = (f32[6,16,24,128]{3,2,1,0:T(8,128)S(1)}, f32[6,16,24,128]{3,2,1,0:T(8,128)}, u32[]{:S(2)}) copy-start(f32[6,16,24,128]{3,2,1,0:T(8,128)} %fields_hbm.1) | copy-start | bytes 3538948
  1.9 0.9 %copy-start.1 = (s32[16,24,128]{2,1,0:T(8,128)S(1)}, s32[16,24,128]{2,1,0:T(8,128)}, u32[]{:S(2)}) copy-start(s32[16,24,128]{2,1,0:T(8,128)} %material_ref.1) | copy-start | bytes 589828
  2.8 0.7 %copy-start.2 = (s32[256]{0:T(256)S(1)}, s32[256]{0:T(256)}, u32[]{:S(2)}) copy-start(s32[256]{0:T(256)} %cell_smem.1) | copy-start | bytes 3076
  3.5 0.7 %copy-start.3 = (s32[256,1]{0,1:T(1,128)S(1)}, s32[256,1]{0,1:T(1,128)}, u32[]{:S(2)}) copy-start(s32[256,1]{0,1:T(1,128)} %param.9) | copy-start | bytes 3076
  4.2 0.7 %copy-start.4 = (f32[16]{0:T(128)S(1)}, f32[16]{0:T(128)}, u32[]{:S(2)}) copy-start(f32[16]{0:T(128)} %permit_ref.1) | copy-start | bytes 196

commit v2 on v1

--- a/solution.py
+++ b/solution.py
@@ -292,19 +292,21 @@
     lax.fori_loop(0, angles // 8, group, tuple(wide))
 
 
-def step_kernel(nx, ny, cx, cy, cz, scale, fields_hbm, material_ref, permit_ref, cell_smem,
-                cell_row, owner_row, out_ref, far_ref,
+def step_kernel(nx, ny, cx, cy, cz, scale, fields_hbm, material_hbm, permit_ref, cell_smem,
+                cell_row, owner_row, new_hbm, far_ref, material_ref, out_ref,
                 grid_x, grid_y, y_out, y_low, y_high, coef_x,
                 gain_x, pivot_x, left_x, right_x, solved_x,
                 coef_y, gain_y, pivot_y, left_y, right_y, solved_y,
                 weight_ref, packed, samples, spread, parts, landed,
-                load_sem, halo_sems, part_sems, *line_refs):
+                load_sem, move_sems, halo_sems, part_sems, *line_refs):
     half_step = COURANT / 2.0
     count = nx * ny
     me = lax.axis_index("gx") * ny + lax.axis_index("gy")
     barrier = pltpu.get_barrier_semaphore()
     load = pltpu.make_async_copy(fields_hbm, grid_x.at[:, pl.ds(1, cx)], load_sem)
     load.start()
+    load_material = pltpu.make_async_copy(material_hbm, material_ref, move_sems.at[0])
+    load_material.start()
     greet_all(count, ny, me, barrier)
     line_x = Line("gx", nx, line_refs[:9])
     line_y = Line("gy", ny, line_refs[9:])
@@ -324,6 +326,7 @@
         coef_x[pl.ds(pl.multiple_of(i * cy, 8), cy), :] = (half_step * half_step) / permit
         return carry
 
+    load_material.wait()
     lax.fori_loop(0, cx, coefs, 0, unroll=2)
     load.wait()
     for slot, member in enumerate(Y_MEMBERS):
@@ -353,7 +356,7 @@
             solved_x[m, i] = now[m]
         return tuple(now)
 
-    lax.fori_loop(0, cx, forward_x, (jnp.zeros((cy, cz), jnp.float32),) * 6)
+    lax.fori_loop(0, cx, forward_x, (jnp.zeros((cy, cz), jnp.float32),) * 6, unroll=2)
     early = min(2, line_x.steps)
     line_x.mat_merge(0)
     sweep_back(cx, gain_x, solved_x)
@@ -408,6 +411,8 @@
             out_ref[m, pl.ds(j, cx, stride=cy), :] = value
             packed[pl.ds(j * 8 + m, cx, stride=cy * 8), :] = value
 
+    save = pltpu.make_async_copy(out_ref, new_hbm, move_sems.at[1])
+    save.start()
     patches = cell_smem.shape[0]
 
     def fetch(q, carry):
@@ -467,6 +472,7 @@
         return carry
 
     lax.fori_loop(1, count, done, 0)
+    save.wait()
 
 
 def line_scratch(count, rows, lanes):
@@ -492,6 +498,7 @@
     patches = patch_cell.shape[0]
     vmem = pl.BlockSpec(memory_space=pltpu.VMEM)
     smem = pl.BlockSpec(memory_space=pltpu.SMEM)
+    hbm = pl.BlockSpec(memory_space=pltpu.HBM)
     x_lines = [pltpu.VMEM((cx, cy, cz), f32)] * 4
     y_lines = [pltpu.VMEM((cy, cx, cz), f32)] * 4
     new_flat, far_field = pl.pallas_call(
@@ -500,9 +507,11 @@
             jax.ShapeDtypeStruct((6, cx * cy, cz), f32),
             jax.ShapeDtypeStruct((12, ANG_DEV), f32),
         ),
-        in_specs=[pl.BlockSpec(memory_space=pltpu.HBM), vmem, smem, smem, vmem, vmem],
-        out_specs=(vmem, vmem),
+        in_specs=[hbm, hbm, smem, smem, vmem, vmem],
+        out_specs=(hbm, vmem),
         scratch_shapes=[
+            pltpu.VMEM((cx, cy, cz), jnp.int32),
+            pltpu.VMEM((6, cx * cy, cz), f32),
             pltpu.VMEM((6, cx + 2, cy, cz), f32),
             pltpu.VMEM((6, (cy + 2) * cx, cz), f32),
             pltpu.VMEM((2, 4, cx, cz), f32),
@@ -521,13 +530,14 @@
             pltpu.VMEM((count * 16, ANG_DEV), f32),
             pltpu.VMEM((count, 16, ANG_DEV), f32),
             pltpu.SemaphoreType.DMA,
+            pltpu.SemaphoreType.DMA((2,)),
             pltpu.SemaphoreType.DMA((3, 4)),
             pltpu.SemaphoreType.DMA((2, count)),
             *line_scratch(nx, cy, cz),
             *line_scratch(ny, cx, cz),
         ],
         compiler_params=pltpu.CompilerParams(
-            collective_id=0, has_side_effects=True, vmem_limit_bytes=40 * 2**20),
+            collective_id=0, has_side_effects=True),
         name="split_step",
     )(fields, material, permittivity, patch_cell, patch_cell[None, :], patch_owner.reshape(1, patches))
     return new_flat.reshape(fields.shape), far_field

time: 50.9 us -> 48.3 us (0.949)
  local copies, waits for them, and re-layouts: 5.82 us -> 2.97 us
    unnamed x12 -> x4, local copies, waits for them, and re-layouts: 5.82 us -> 2.97 us
where the time goes in v2:
time: 48.3 us; the launch traced here: 48.1 us
  Pallas kernels  44.5 us (92%)
  local copies, waits for them, and re-layouts  2.97 us (6%)
  between operations  0.65 us (1%)
    pallas_call x1, Pallas kernels, local(): pl.pallas_call(functools.partial(step_kernel, nx, ny, cx, cy, cz, 1.0 / m...  44.5 us
    unnamed x4, local copies, waits for them, and re-layouts  2.97 us

profile of v2, /device:TPU:0, one launch (start us, length us, event | category | flops | bytes accessed | tf_op | source)
XLA Modules:
  0.0 48.1 jit_solution(7468191186934886865)
XLA Ops:
  0.6 44.5 %split_step.1 = (f32[6,384,128]{2,1,0:T(8,128)}, f32[12,128]{1,0:T(8,128)}) custom-call(f32[6,16,24,128]{3,2,1,0:T(8,128)} %fields_hbm.1, s32[16,24,128]{2,1,0:T(8,128)} %material_hbm.1, f32[16]{0:T(128)} %permit_ref.1, s32[256]{0:T(256)} %cell_smem.1, s32[1,256]{1,0:T(1,128)} %bitcast.4, s32[1,256]{1,0:T(1,128)} %bitcast.5), custom_call_target="tpu_custom_call" | custom-call | tf_op jit(solution)/shard_map/split_step/pallas_call | solution.py:504
  45.1 0.0 copy-start
  45.1 2.4 %copy.9 = f32[6,16,24,128]{3,2,1,0:T(8,128)} copy(f32[6,16,24,128]{3,2,1,0:T(8,128)} %bitcast.3) | data formatting | bytes 2359296
  47.5 0.0 copy-done
  47.5 0.6 %copy.10 = f32[12,128]{1,0:T(8,128)} copy(f32[12,128]{1,0:T(8,128)S(1)} %copy-done) | data formatting | bytes 12288
Async XLA Ops:
  45.1 2.4 %copy-start = (f32[12,128]{1,0:T(8,128)S(1)}, f32[12,128]{1,0:T(8,128)}, u32[]{:S(2)}) copy-start(f32[12,128]{1,0:T(8,128)} %get-tuple-element.9) | copy-start | bytes 18436
